TPU v7x, 128 devices: a whole 4x4x4 slice. The times are simulated.
128 devices in a mesh: comp: 16 (over y, x), port: 8 (over z, core).
Axes of the slice: x: 4, y: 4, z: 4, core: 2. Of those that a mesh axis runs over, the one named last changes fastest.
Arguments:
- mode_shapes: bfloat16 [256, 8192, 128], P('comp', 'port'), may hold values from -0.0625 to 0.0625
- block_values: bfloat16 [256, 64, 3, 128, 128], P('comp', 'port'), may hold values from -1.1953125 to 1.1953125
- block_offsets: int32 [256, 64, 3], P('comp', 'port'), may hold values from -2 to 2
- conductance: float32 [256, 8192], P('comp', 'port'), may hold values from 0.1 to 10
- capacity: float32 [256, 8192], P('comp', 'port'), may hold values from 0.1 to 10
- coupling: bfloat16 [256, 4, 128, 256], P('comp'), may hold values from -384 to 384
- surface_blocks: int32 [256, 4], P('comp'), may hold values from 0 to 63, as said below
- port_ids: int32 [256, 4], P('comp'), may hold values from 0 to 255, as said below
- port_counts: int32 [256], P('comp'), may hold values from 1 to 4
- boundary: float32 [256, 256, 256], P(('comp', 'port')), may hold values from -3 to 3
Outputs:
- modal_conductance: float32 [256, 128, 128], P('comp', 'port')
- modal_capacity: float32 [256, 128, 128], P('comp', 'port')
- interface: float32 [256, 256, 256], P(('comp', 'port'))
Inputs may be any that keep to these rules, and one draw needn't show every extreme that they name: Slot s of component c has its surface cells on index surface_blocks[c, s] // 8 of port; its port is owned on index (port_ids[c, s] // 2) % 8 of port. Among the slots of the components of one index of comp, padding slots included, at most 2 lie on one index of port and name ports owned on one given index of port, and in every index of comp one such pair holds exactly 2. `port_ids`: port p is stored on device p // 2 of comp+port. Among the slots of the components of one index of comp, padding slots included, at most 2 name ports stored on one given device, and in every index of comp some device receives exactly 2; see surface_blocks for the other bound.
All inputs are finite; a program needn't handle non-finite values.
Results may differ from a plain program's by a relative error of at most 0.0008.
Values may be sent and summed in bfloat16 or wider, within the bound.
A program may use at most 320 MiB of HBM per device.

v0:
```python
import jax
import jax.numpy as jnp
from jax import lax
from jax.sharding import PartitionSpec as P


def padded_2(value, sides, width):
    for axis, dim in sides:
        size, length = (lax.axis_size(axis), value.shape[dim])
        up = [(i, (i + 1) % size) for i in range(size - 1)]
        down = [(j, i) for i, j in up]
        last = lax.slice_in_dim(value, length - width, length, axis=dim)
        first = lax.slice_in_dim(value, 0, width, axis=dim)
        before = lax.ppermute(last, axis, up)
        after = lax.ppermute(first, axis, down)
        value = jnp.concatenate([before, value, after], axis=dim)
    return value


def split_up(value, dim, length):
    before, after = (value.shape[:dim], value.shape[dim + 1 :])
    return jnp.moveaxis(value.reshape(*before, length, -1, *after), dim, 0)


def sum_at_owner(value, axis, dim):
    pieces = split_up(value, dim, lax.axis_size(axis))
    arrived = lax.all_to_all(pieces, axis, split_axis=0, concat_axis=0, tiled=True)
    return arrived.sum(axis=0)


def side_by_side(arrays, axis, dim, along):
    ends, at = ([], 0)
    for a in arrays[:-1]:
        at += a.shape[along]
        ends.append(at)
    both = jnp.concatenate(arrays, axis=along)
    return tuple(jnp.split(sum_at_owner(both, axis, dim), ends, axis=along))


def shards(
    mode_shapes,
    block_values,
    block_offsets,
    conductance,
    capacity,
    coupling,
    surface_blocks,
    port_ids,
    port_counts,
    boundary,
):
    comp_local, cell_rows, mode_count = mode_shapes.shape
    block_rows = block_values.shape[1]
    stored_count = block_values.shape[2]
    block_size = block_values.shape[3]
    slot_count = coupling.shape[1]
    port_block = coupling.shape[3]
    ports_owned = boundary.shape[0]
    port_size = lax.axis_size("port")
    comp_size = lax.axis_size("comp")
    my_port = lax.axis_index("port")
    shaped = mode_shapes.reshape(comp_local, block_rows, block_size, mode_count)
    padded = padded_2(shaped, (("port", 1),), 2)
    summed = conductance.reshape(comp_local, block_rows, block_size, 1) * shaped.astype(jnp.float32)
    zero_block = jnp.zeros_like(block_values[:, :, 0])
    for offset_value in range(-2, 3):
        window = padded[:, 2 + offset_value : 2 + offset_value + block_rows]
        for stored in range(stored_count):
            hitting = (block_offsets[:, :, stored] == offset_value)[:, :, None, None]
            masked = jnp.where(hitting, block_values[:, :, stored], zero_block)
            summed = summed + jnp.einsum(
                "crij,crjm->crim", masked, window, preferred_element_type=jnp.float32
            )
    conducted = summed.astype(jnp.bfloat16)
    weighted = (
        capacity.reshape(comp_local, block_rows, block_size, 1) * shaped.astype(jnp.float32)
    ).astype(jnp.bfloat16)
    cond_part = jnp.einsum("crbm,crbn->cmn", shaped, conducted, preferred_element_type=jnp.float32)
    heat_part = jnp.einsum("crbm,crbn->cmn", shaped, weighted, preferred_element_type=jnp.float32)
    modal_conductance, modal_capacity = side_by_side((cond_part, heat_part), "port", 1, 0)
    slot_total = comp_local * slot_count
    surface_flat = surface_blocks.reshape(-1)
    ports_flat = port_ids.reshape(-1)
    shard_of = surface_flat // block_rows
    owner_port = ports_flat // ports_owned % port_size
    cell_id = shard_of * port_size + owner_port
    slot_order = jnp.arange(slot_total, dtype=jnp.int32)
    earlier = (cell_id[:, None] == cell_id[None, :]) & (slot_order[:, None] > slot_order[None, :])
    rank_in = jnp.sum(earlier.astype(jnp.int32), axis=1)
    comp_of = slot_order // slot_count
    slot_of = slot_order % slot_count
    alive = (slot_of < port_counts[comp_of]) & (shard_of == my_port)
    capacity_slots = max(2, (slot_total - 1) // (port_size * port_size) + 1)
    own_cap = max(2, (port_size * capacity_slots - 1) // comp_size + 1)
    position = owner_port * capacity_slots + rank_in
    buffer_len = port_size * capacity_slots
    chosen = (position[None, :] == jnp.arange(buffer_len, dtype=jnp.int32)[:, None]) & alive[
        None, :
    ]
    present = jnp.any(chosen, axis=1)
    source = jnp.sum(jnp.where(chosen, slot_order[None, :], 0), axis=1)
    target = comp_of[source] * block_rows + surface_flat[source] % block_rows
    row_pick = (
        target[:, None] == jnp.arange(comp_local * block_rows, dtype=jnp.int32)[None, :]
    ).astype(jnp.bfloat16)
    rows_sel = jnp.einsum(
        "qr,rbm->qbm",
        row_pick,
        shaped.reshape(comp_local * block_rows, block_size, mode_count),
        preferred_element_type=jnp.float32,
    ).astype(jnp.bfloat16)
    slot_pick = (source[:, None] == slot_order[None, :]).astype(jnp.bfloat16)
    couple_sel = jnp.einsum(
        "qs,sbp->qbp",
        slot_pick,
        coupling.reshape(slot_total, block_size, port_block),
        preferred_element_type=jnp.float32,
    ).astype(jnp.bfloat16)
    factors = jnp.einsum(
        "qbm,qbp->qmp", rows_sel, couple_sel, preferred_element_type=jnp.float32
    ).astype(jnp.bfloat16)
    factors = jnp.where(present[:, None, None], factors, jnp.zeros_like(factors))
    sent_ids = jnp.where(present, ports_flat[source], -1)
    received, received_ids = (
        lax.all_to_all(
            factors.reshape(port_size, capacity_slots, mode_count, port_block),
            "port",
            split_axis=0,
            concat_axis=0,
            tiled=True,
        ),
        lax.all_to_all(
            sent_ids.reshape(port_size, capacity_slots),
            "port",
            split_axis=0,
            concat_axis=0,
            tiled=True,
        ),
    )
    received = received.reshape(-1, mode_count, port_block)
    received_ids = received_ids.reshape(-1)
    owned_range = jnp.arange(ports_owned, dtype=jnp.int32)
    valid = received_ids >= 0
    comp_target = jnp.where(valid, received_ids // (port_size * ports_owned), -1)
    row_count = received_ids.shape[0]
    row_order = jnp.arange(row_count, dtype=jnp.int32)
    before = (comp_target[:, None] == comp_target[None, :]) & (
        row_order[:, None] > row_order[None, :]
    )
    rank_target = jnp.sum(before.astype(jnp.int32), axis=1)
    slot_pos = comp_target * own_cap + rank_target
    pick = (slot_pos[None, :] == jnp.arange(comp_size * own_cap, dtype=jnp.int32)[:, None]) & valid[
        None, :
    ]
    packed = jnp.einsum(
        "kr,rmp->kmp", pick.astype(jnp.bfloat16), received, preferred_element_type=jnp.float32
    ).astype(jnp.bfloat16)
    packed_ids = jnp.where(
        jnp.any(pick, axis=1), jnp.sum(jnp.where(pick, received_ids[None, :], 0), axis=1), -1
    ).astype(jnp.int32)
    part_factors = lax.all_to_all(
        packed.reshape(comp_size, own_cap, mode_count, port_block),
        "comp",
        split_axis=0,
        concat_axis=0,
        tiled=True,
    )
    part_ids = lax.all_to_all(
        packed_ids.reshape(comp_size, own_cap), "comp", split_axis=0, concat_axis=0, tiled=True
    )
    weight = (
        (part_ids[:, :, None] % ports_owned == owned_range[None, None, :])
        & (part_ids[:, :, None] >= 0)
    ).astype(jnp.float32)
    squares = jnp.einsum(
        "nkmp,nkmq->nkpq", part_factors, part_factors, preferred_element_type=jnp.float32
    ) * (1.0 / mode_count)
    settled = jnp.einsum("nko,nkpq->kopq", weight, squares, precision=lax.Precision.HIGHEST)
    assembled = jnp.sum(settled, axis=0)
    interface = boundary + assembled
    return (modal_conductance, modal_capacity, interface)


def solution(mesh):
    in_specs = (
        P("comp", "port", None),
        P("comp", "port", None, None, None),
        P("comp", "port", None),
        P("comp", "port"),
        P("comp", "port"),
        P("comp", None, None, None),
        P("comp", None),
        P("comp", None),
        P("comp"),
        P(("comp", "port"), None, None),
    )
    out_specs = (P("comp", "port", None), P("comp", "port", None), P(("comp", "port"), None, None))
    return jax.shard_map(shards, mesh=mesh, in_specs=in_specs, out_specs=out_specs, check_vma=False)
```

profile of v0, /device:TPU:1, one launch (start us, length us, event | category | flops | bytes accessed | tf_op | source)
XLA Modules:
  0.0 251.4 jit_solution(16966654183424652384)
XLA Ops:
  0.7 2.7 %fusion.175 = (bf16[16,2,128,128]{3,2,1,0:T(8,128)(2,1)}, bf16[16,2,128,128]{3,2,1,0:T(8,128)(2,1)S(1)}) fusion(bf16[16,8,128,128]{3,2,1,0:T(8,128)(2,1)} %bitcast.128), kind=kLoop, calls=%fused_computation.246 | loop fusion | bytes 4194304 | tf_op jit(solution)/shard_map/slice | solution.py:12
  3.4 4.9 %collective-permute-start = (bf16[16,2,128,128]{3,2,1,0:T(8,128)(2,1)}, bf16[16,2,128,128]{3,2,1,0:T(8,128)(2,1)S(1)}, u32[]{:S(2)}, u32[]{:S(2)}) collective-permute-start(bf16[16,2,128,128]{3,2,1,0:T(8,128)(2,1)} %get-tuple-element.19), channel_id=1, source_target_pairs={{0,1},{1,2},{2,3},{3,4},{4,5},{5,6},{6,7},{8,9},{9,10},{10,11},{11... | collective-permute-start | bytes 3145736 | tf_op jit(solution)/shard_map/ppermute | solution.py:14
  8.3 1.9 collective-permute-start.1
  10.4 0.1 reshape.565
  10.6 0.1 reshape.564
  10.7 0.8 gather_fusion
  11.5 0.2 convert_reduce_fusion
  11.7 0.1 select_reduce_fusion.1
  11.8 0.1 fusion.120
  11.9 0.7 gather_fusion.1
  12.6 0.7 select_n.253
  13.3 5.5 %all-to-all-start.1 = ((s32[8,1,2]{2,1,0:T(1,128)}), s32[8,1,2]{2,1,0:T(1,128)S(1)}, u32[]{:S(2)}, u32[]{:S(2)}) async-start(s32[8,1,2]{2,1,0:T(1,128)} %bitcast.30), calls=%async_computation.1 | async-start | bytes 8192 | tf_op jit(solution)/shard_map/all_to_all | solution.py:132
  18.8 0.7 gather_fusion.3
  19.5 0.1 copy.102
  19.6 0.1 copy.106
  19.7 0.1 copy.112
  19.8 0.1 copy.115
  19.8 0.1 copy.100
  19.9 0.1 copy.105
  20.0 0.1 copy.111
  20.3 0.1 copy.104
  20.7 8.1 %fusion.33 = f32[16,8,128,128]{3,2,1,0:T(8,128)} fusion(bf16[16,8,128,128]{3,2,1,0:T(8,128)(2,1)} %bitcast.129, pred[16,8]{1,0:T(8,128)(4,1)S(1)} %copy.108, bf16[16,8,3,128,128]{4,3,2,1,0:T(8,128)(2,1)} %param.11), kind=kOutput, calls=%fused_computation.52 | convolution fusion | flops 538968064 | bytes 16777344 | tf_op jit(solution)/shard_map/crij,crjm->crim/dot_general | solution.py:71
  28.9 6.8 %fusion.38 = f32[16,8,128,128]{3,2,1,0:T(8,128)} fusion(bf16[16,8,128,128]{3,2,1,0:T(8,128)(2,1)S(1)} %bitcast.133, pred[16,8]{1,0:T(8,128)(4,1)S(1)} %copy.107, bf16[16,8,3,128,128]{4,3,2,1,0:T(8,128)(2,1)} %param.11), kind=kOutput, calls=%fused_computation.62 | convolution fusion | flops 538968064 | bytes 16777344 | tf_op jit(solution)/shard_map/crij,crjm->crim/dot_general | solution.py:71
  35.8 7.7 %fusion.100 = f32[16,128,128]{2,1,0:T(8,128)} fusion(bf16[16,8,128,128]{3,2,1,0:T(8,128)(2,1)} %bitcast.130, f32[16,8,128]{2,1,0:T(8,128)S(1)} %bitcast.155), kind=kOutput, calls=%fused_computation.124 | convolution fusion | flops 543162368 | bytes 5308416 | tf_op jit(solution)/shard_map/crbm,crbn->cmn/dot_general | solution.py:79
  43.5 0.7 gather_fusion.2
  44.2 4.7 %fusion.96 = bf16[16,128,256]{2,0,1:T(8,128)(2,1)S(1)} fusion(bf16[64,128,256]{2,1,0:T(8,128)(2,1)} %bitcast.150, s32[16]{0:T(128)S(1)} %select_reduce_fusion.1), kind=kOutput, calls=%fused_computation.121 | convolution fusion | flops 67634176 | bytes 5242944 | tf_op jit(solution)/shard_map/qs,sbp->qbp/dot_general | solution.py:113
  48.9 2.4 fusion.106
  51.3 1.6 fusion.99
  52.9 0.5 broadcast.688
  53.4 0.7 reduce.3
  54.2 0.2 convert_reduce_fusion.1
  54.4 0.1 fusion.124
  54.5 0.1 select_reduce_fusion
  54.6 0.7 select_n.258
  55.3 6.8 %all-to-all-start.2 = ((s32[16,1,2]{2,1,0:T(1,128)}), s32[16,1,2]{2,1,0:T(1,128)S(1)}, u32[]{:S(2)}, u32[]{:S(2)}) async-start(s32[16,1,2]{2,1,0:T(1,128)} %bitcast.31), calls=%async_computation.2 | async-start | bytes 16384 | tf_op jit(solution)/shard_map/all_to_all | solution.py:168
  62.1 8.9 %fusion.28 = f32[16,8,128,128]{3,2,1,0:T(8,128)} fusion(pred[16,8]{1,0:T(8,128)(4,1)S(1)} %copy.106, bf16[16,8,3,128,128]{4,3,2,1,0:T(8,128)(2,1)} %param.11, bf16[16,8,128,128]{3,2,1,0:T(8,128)(2,1)} %bitcast.131, bf16[16,2,128,128]{3,2,1,0:T(8,128)(2,1)S(1)} %collective-permute-done), kind=kOutput, calls=%fused_computation.42 | convolution fusion | flops 541065216 | bytes 17825920 | tf_op jit(solution)/shard_map/crij,crjm->crim/dot_general | solution.py:71
  71.0 5.8 %fusion.27 = f32[16,8,128,128]{3,2,1,0:T(8,128)} fusion(pred[16,8]{1,0:T(8,128)(4,1)S(1)} %copy.102, bf16[16,8,3,128,128]{4,3,2,1,0:T(8,128)(2,1)} %param.11, bf16[16,2,128,128]{3,2,1,0:T(8,128)(2,1)S(1)} %collective-permute-done, bf16[16,8,128,128]{3,2,1,0:T(8,128)(2,1)S(1)} %bitcast.135), kind=kOutput, calls=%fused_computation.41 | convolution fusion | flops 541065216 | bytes 17825920 | tf_op jit(solution)/shard_map/crij,crjm->crim/dot_general | solution.py:71
  76.9 4.0 %fusion.29 = f32[16,8,128,128]{3,2,1,0:T(8,128)} fusion(pred[16,8]{1,0:T(8,128)(4,1)S(1)} %copy.112, bf16[16,8,3,128,128]{4,3,2,1,0:T(8,128)(2,1)S(1)} %bitcast.147, bf16[16,8,128,128]{3,2,1,0:T(8,128)(2,1)S(1)} %bitcast.136, bf16[16,2,128,128]{3,2,1,0:T(8,128)(2,1)S(1)} %collective-permute-done.1), kind=kOutput, calls=%fused_computation.43 | convolution fusion | flops 541065216 | bytes 17827840 | tf_op jit(solution)/shard_map/crij,crjm->crim/dot_general | solution.py:71
  80.9 4.0 %fusion.30 = f32[16,8,128,128]{3,2,1,0:T(8,128)} fusion(pred[16,8]{1,0:T(8,128)(4,1)S(1)} %copy.115, bf16[16,8,3,128,128]{4,3,2,1,0:T(8,128)(2,1)S(1)} %bitcast.147, bf16[16,2,128,128]{3,2,1,0:T(8,128)(2,1)S(1)} %collective-permute-done.1, bf16[16,8,128,128]{3,2,1,0:T(8,128)(2,1)S(1)} %bitcast.137), kind=kOutput, calls=%fused_computation.44 | convolution fusion | flops 541065216 | bytes 17827840 | tf_op jit(solution)/shard_map/crij,crjm->crim/dot_general | solution.py:71
  84.9 4.1 %fusion.31 = f32[16,8,128,128]{3,2,1,0:T(8,128)} fusion(pred[16,8]{1,0:T(8,128)(4,1)S(1)} %copy.100, bf16[16,8,3,128,128]{4,3,2,1,0:T(8,128)(2,1)S(1)} %bitcast.147, bf16[16,2,128,128]{3,2,1,0:T(8,128)(2,1)S(1)} %collective-permute-done, bf16[16,8,128,128]{3,2,1,0:T(8,128)(2,1)S(1)} %bitcast.138), kind=kOutput, calls=%fused_computation.50 | convolution fusion | flops 541065216 | bytes 17827840 | tf_op jit(solution)/shard_map/crij,crjm->crim/dot_general | solution.py:71
  88.9 4.1 %fusion.32 = f32[16,8,128,128]{3,2,1,0:T(8,128)} fusion(pred[16,8]{1,0:T(8,128)(4,1)S(1)} %copy.105, bf16[16,8,3,128,128]{4,3,2,1,0:T(8,128)(2,1)S(1)} %bitcast.147, bf16[16,8,128,128]{3,2,1,0:T(8,128)(2,1)S(1)} %bitcast.139, bf16[16,2,128,128]{3,2,1,0:T(8,128)(2,1)S(1)} %collective-permute-done), kind=kOutput, calls=%fused_computation.51 | convolution fusion | flops 541065216 | bytes 17827840 | tf_op jit(solution)/shard_map/crij,crjm->crim/dot_general | solution.py:71
  93.0 4.0 %fusion.34 = f32[16,8,128,128]{3,2,1,0:T(8,128)} fusion(pred[16,8]{1,0:T(8,128)(4,1)S(1)} %copy.111, bf16[16,8,3,128,128]{4,3,2,1,0:T(8,128)(2,1)S(1)} %bitcast.147, bf16[16,8,128,128]{3,2,1,0:T(8,128)(2,1)S(1)} %bitcast.140, bf16[16,2,128,128]{3,2,1,0:T(8,128)(2,1)S(1)} %collective-permute-done.1), kind=kOutput, calls=%fused_computation.53 | convolution fusion | flops 541065216 | bytes 17827840 | tf_op jit(solution)/shard_map/crij,crjm->crim/dot_general | solution.py:71
  97.0 4.0 %fusion.35 = f32[16,8,128,128]{3,2,1,0:T(8,128)} fusion(pred[16,8]{1,0:T(8,128)(4,1)S(1)} %copy.114, bf16[16,8,3,128,128]{4,3,2,1,0:T(8,128)(2,1)S(1)} %bitcast.147, bf16[16,2,128,128]{3,2,1,0:T(8,128)(2,1)S(1)} %collective-permute-done.1, bf16[16,8,128,128]{3,2,1,0:T(8,128)(2,1)S(1)} %bitcast.141), kind=kOutput, calls=%fused_computation.54 | convolution fusion | flops 541065216 | bytes 17827840 | tf_op jit(solution)/shard_map/crij,crjm->crim/dot_general | solution.py:71
  101.0 4.0 %fusion.36 = f32[16,8,128,128]{3,2,1,0:T(8,128)} fusion(pred[16,8]{1,0:T(8,128)(4,1)S(1)} %copy.99, bf16[16,8,3,128,128]{4,3,2,1,0:T(8,128)(2,1)S(1)} %bitcast.147, bf16[16,2,128,128]{3,2,1,0:T(8,128)(2,1)S(1)} %collective-permute-done, bf16[16,8,128,128]{3,2,1,0:T(8,128)(2,1)S(1)} %bitcast.142), kind=kOutput, calls=%fused_computation.60 | convolution fusion | flops 541065216 | bytes 17827840 | tf_op jit(solution)/shard_map/crij,crjm->crim/dot_general | solution.py:71
  104.9 4.0 %fusion.37 = f32[16,8,128,128]{3,2,1,0:T(8,128)} fusion(pred[16,8]{1,0:T(8,128)(4,1)S(1)} %copy.104, bf16[16,8,3,128,128]{4,3,2,1,0:T(8,128)(2,1)S(1)} %bitcast.147, bf16[16,8,128,128]{3,2,1,0:T(8,128)(2,1)S(1)} %bitcast.143, bf16[16,2,128,128]{3,2,1,0:T(8,128)(2,1)S(1)} %collective-permute-done), kind=kOutput, calls=%fused_computation.61 | convolution fusion | flops 541065216 | bytes 17827840 | tf_op jit(solution)/shard_map/crij,crjm->crim/dot_general | solution.py:71
  108.9 4.0 %fusion.39 = f32[16,8,128,128]{3,2,1,0:T(8,128)} fusion(pred[16,8]{1,0:T(8,128)(4,1)S(1)} %copy.110, bf16[16,8,3,128,128]{4,3,2,1,0:T(8,128)(2,1)S(1)} %bitcast.147, bf16[16,8,128,128]{3,2,1,0:T(8,128)(2,1)S(1)} %bitcast.144, bf16[16,2,128,128]{3,2,1,0:T(8,128)(2,1)S(1)} %collective-permute-done.1), kind=kOutput, calls=%fused_computation.63 | convolution fusion | flops 541065216 | bytes 17827840 | tf_op jit(solution)/shard_map/crij,crjm->crim/dot_general | solution.py:71
  112.9 4.0 %fusion.40 = f32[16,8,128,128]{3,2,1,0:T(8,128)} fusion(pred[16,8]{1,0:T(8,128)(4,1)S(1)} %copy.113, bf16[16,8,3,128,128]{4,3,2,1,0:T(8,128)(2,1)S(1)} %bitcast.147, bf16[16,2,128,128]{3,2,1,0:T(8,128)(2,1)S(1)} %collective-permute-done.1, bf16[16,8,128,128]{3,2,1,0:T(8,128)(2,1)S(1)} %bitcast.145), kind=kOutput, calls=%fused_computation.64 | convolution fusion | flops 541065216 | bytes 17827840 | tf_op jit(solution)/shard_map/crij,crjm->crim/dot_general | solution.py:71
  116.9 5.1 %all-to-all-start.3 = ((bf16[8,2,128,256]{3,2,1,0:T(8,128)(2,1)}), bf16[8,2,128,256]{3,2,1,0:T(8,128)(2,1)S(1)}, u32[]{:S(2)}, u32[]{:S(2)}) async-start(bf16[8,2,128,256]{3,2,1,0:T(8,128)(2,1)} %bitcast.39), calls=%async_computation.3 | async-start | bytes 2097152 | tf_op jit(solution)/shard_map/all_to_all | solution.py:125
  122.0 48.2 %fusion.103 = f32[16,128,128]{2,1,0:T(8,128)S(1)} fusion(bf16[16,8,128,128]{3,2,1,0:T(8,128)(2,1)} %bitcast.132, f32[16,8,128,128]{3,2,1,0:T(8,128)} %fusion.30, f32[16,8,128,128]{3,2,1,0:T(8,128)} %fusion.35, f32[16,8,128,128]{3,2,1,0:T(8,128)} %fusion.40, f32[16,8,128,128]{3,2,1,0:T(8,128)} %fusion.29, f32[16,8,128,128]{3,2,1,0:T(8,128)} %fusion.34, ...), kind=kOutput, calls=%fused_computation.125 | convolution fusion | flops 1113587712 | bytes 135331968 | tf_op jit(solution)/shard_map/crbm,crbn->cmn/dot_general | solution.py:78
  170.2 0.1 pad_maximum_fusion.2
  170.3 1.5 copy.169
  171.9 4.8 %all-to-all-start = ((f32[8,32,16,128]{3,2,1,0:T(8,128)}), f32[8,32,16,128]{3,2,1,0:T(8,128)S(1)}, u32[]{:S(2)}, u32[]{:S(2)}) async-start(f32[8,32,16,128]{3,2,1,0:T(8,128)} %bitcast.148), calls=%async_computation | async-start | bytes 4194304 | tf_op jit(solution)/shard_map/all_to_all | solution.py:27
  176.7 2.2 convolution_convert_fusion
  178.9 4.1 %reshape.570 = bf16[16,2,128,256]{3,1,0,2:T(2,128)(2,1)} reshape(bf16[32,128,256]{2,0,1:T(8,128)(2,1)} %convolution_convert_fusion) | data formatting | bytes 4194304 | tf_op jit(solution)/shard_map/reshape | solution.py:162
  183.0 4.8 %copy.129 = bf16[16,2,128,256]{3,1,2,0:T(2,128)(2,1)} copy(bf16[16,2,128,256]{3,1,0,2:T(2,128)(2,1)} %reshape.570) | data formatting | bytes 4194304 | tf_op jit(solution)/shard_map/reshape | solution.py:162
  187.9 15.2 %all-to-all-done = f32[8,32,16,128]{3,2,1,0:T(8,128)S(1)} async-done(((f32[8,32,16,128]{3,2,1,0:T(8,128)}), f32[8,32,16,128]{3,2,1,0:T(8,128)S(1)}, u32[]{:S(2)}, u32[]{:S(2)}) %all-to-all-start) | async-done | bytes 2097184 | tf_op jit(solution)/shard_map/all_to_all | solution.py:27
  203.0 1.3 copy-done.5
  204.4 6.9 %all-to-all-start.4 = ((bf16[16,2,128,256]{3,1,2,0:T(2,128)(2,1)}), bf16[16,2,128,256]{3,1,2,0:T(2,128)(2,1)S(1)}, u32[]{:S(2)}, u32[]{:S(2)}) async-start(bf16[16,2,128,256]{3,1,2,0:T(2,128)(2,1)} %copy.129), calls=%async_computation.4 | async-start | bytes 4194304 | tf_op jit(solution)/shard_map/all_to_all | solution.py:161
  211.4 1.8 reduce_sum.51
  213.1 0.7 fusion.176
  213.9 27.4 %all-to-all-done.4 = bf16[16,2,128,256]{3,1,2,0:T(2,128)(2,1)S(1)} async-done(((bf16[16,2,128,256]{3,1,2,0:T(2,128)(2,1)}), bf16[16,2,128,256]{3,1,2,0:T(2,128)(2,1)S(1)}, u32[]{:S(2)}, u32[]{:S(2)}) %all-to-all-start.4) | async-done | bytes 2097184 | tf_op jit(solution)/shard_map/all_to_all | solution.py:161
  241.2 1.3 broadcast_multiply_fusion
  242.5 8.0 %fusion.112 = f32[2,256,256]{2,0,1:T(2,128)S(1)} fusion(f32[16,2,256,256]{3,2,1,0:T(8,128)S(1)} %broadcast_multiply_fusion, f32[2,256,256]{2,1,0:T(8,128)S(1)} %copy-done.7, pred[16,2]{0,1:T(4,128)(4,1)S(1)} %bitcast_compare_fusion, s32[16,2]{0,1:T(2,128)S(1)} %and_select_fusion.2), kind=kOutput, calls=%fused_computation.128 | convolution fusion | flops 50462848 | bytes 9437344 | tf_op jit(solution)/shard_map/nko,nkpq->kopq/dot_general | solution.py:178
  250.5 0.8 copy.134
  (67 shorter events, 1.2 us)
Async XLA Ops:
  0.6 10.0 %copy-start = (s32[16]{0:T(128)S(1)}, s32[16]{0:T(128)}, u32[]{:S(2)}) copy-start(s32[16]{0:T(128)} %param.18) | copy-start | bytes 196
  0.6 9.6 %copy-start.11 = (s32[16,4]{0,1:T(4,128)S(1)}, s32[16,4]{0,1:T(4,128)}, u32[]{:S(2)}) copy-start(s32[16,4]{0,1:T(4,128)} %param.16) | copy-start | bytes 772
  0.7 9.8 %copy-start.12 = (s32[16,4]{0,1:T(4,128)S(1)}, s32[16,4]{0,1:T(4,128)}, u32[]{:S(2)}) copy-start(s32[16,4]{0,1:T(4,128)} %param.17) | copy-start | bytes 772
  0.7 18.8 %copy-start.10 = (s32[16,8,3]{0,1,2:T(8,128)S(1)}, s32[16,8,3]{0,1,2:T(8,128)}, u32[]{:S(2)}) copy-start(s32[16,8,3]{0,1,2:T(8,128)} %param.12) | copy-start | bytes 4612
  3.4 58.6 %collective-permute-start = (bf16[16,2,128,128]{3,2,1,0:T(8,128)(2,1)}, bf16[16,2,128,128]{3,2,1,0:T(8,128)(2,1)S(1)}, u32[]{:S(2)}, u32[]{:S(2)}) collective-permute-start(bf16[16,2,128,128]{3,2,1,0:T(8,128)(2,1)} %get-tuple-element.19), channel_id=1, source_target_pairs={{0,1},{1,2},{2,3},{3,4},{4,5},{5,6},{6,7},{8,9},{9,10},{10,11},{11... | collective-permute-start | bytes 3145736 | tf_op jit(solution)/shard_map/ppermute | solution.py:14
  8.3 68.5 %collective-permute-start.1 = (bf16[16,2,128,128]{3,2,1,0:T(8,128)(2,1)S(1)}, bf16[16,2,128,128]{3,2,1,0:T(8,128)(2,1)S(1)}, u32[]{:S(2)}, u32[]{:S(2)}) collective-permute-start(bf16[16,2,128,128]{3,2,1,0:T(8,128)(2,1)S(1)} %get-tuple-element.20), channel_id=1, source_target_pairs={{1,0},{2,1},{3,2},{4,3},{5,4},{6,5},{7,6},{9,8},{10,9},{11,10},{12... | collective-permute-start | bytes 3145736 | tf_op jit(solution)/shard_map/ppermute | solution.py:15
  13.3 39.6 %all-to-all-start.1 = ((s32[8,1,2]{2,1,0:T(1,128)}), s32[8,1,2]{2,1,0:T(1,128)S(1)}, u32[]{:S(2)}, u32[]{:S(2)}) async-start(s32[8,1,2]{2,1,0:T(1,128)} %bitcast.30), calls=%async_computation.1 | async-start | bytes 8192 | tf_op jit(solution)/shard_map/all_to_all | solution.py:132
  20.7 8.1 %copy-start.2 = (bf16[16,1024,128]{2,1,0:T(8,128)(2,1)S(1)}, bf16[16,1024,128]{2,1,0:T(8,128)(2,1)}, u32[]{:S(2)}) copy-start(bf16[16,1024,128]{2,1,0:T(8,128)(2,1)} %param.10) | copy-start | bytes 12582916
  28.9 6.9 %copy-start.8 = (f32[16,1024]{1,0:T(8,128)S(1)}, f32[16,1024]{1,0:T(8,128)}, u32[]{:S(2)}) copy-start(f32[16,1024]{1,0:T(8,128)} %param.14) | copy-start | bytes 196612
  44.2 4.7 %copy-start.3 = (bf16[16,1024,128]{2,1,0:T(8,128)(2,1)S(1)}, bf16[16,1024,128]{2,1,0:T(8,128)(2,1)}, u32[]{:S(2)}) copy-start(bf16[16,1024,128]{2,1,0:T(8,128)(2,1)} %param.10) | copy-start | bytes 12582916
  48.9 4.0 %copy-start.9 = (f32[16,1024]{1,0:T(8,128)S(1)}, f32[16,1024]{1,0:T(8,128)}, u32[]{:S(2)}) copy-start(f32[16,1024]{1,0:T(8,128)} %param.13) | copy-start | bytes 196612
  55.3 61.6 %all-to-all-start.2 = ((s32[16,1,2]{2,1,0:T(1,128)}), s32[16,1,2]{2,1,0:T(1,128)S(1)}, u32[]{:S(2)}, u32[]{:S(2)}) async-start(s32[16,1,2]{2,1,0:T(1,128)} %bitcast.31), calls=%async_computation.2 | async-start | bytes 16384 | tf_op jit(solution)/shard_map/all_to_all | solution.py:168
  62.0 9.0 %copy-start.4 = (bf16[16,1024,128]{2,1,0:T(8,128)(2,1)S(1)}, bf16[16,1024,128]{2,1,0:T(8,128)(2,1)}, u32[]{:S(2)}) copy-start(bf16[16,1024,128]{2,1,0:T(8,128)(2,1)} %param.10) | copy-start | bytes 12582916
  62.0 14.8 %slice-start = ((s8[12582912]{0:T(1024)(128)(4,1)}), s8[4194304]{0:T(1024)(128)(4,1)S(1)}, s32[]{:S(2)}) async-start(s8[12582912]{0:T(1024)(128)(4,1)} %bitcast.146), calls=%async_computation.5 | async-start | bytes 8388608
  62.1 14.8 %slice-start.1 = ((s8[12582912]{0:T(1024)(128)(4,1)}), s8[4194304]{0:T(1024)(128)(4,1)S(1)}, s32[]{:S(2)}) async-start(s8[12582912]{0:T(1024)(128)(4,1)} %bitcast.146), calls=%async_computation.6 | async-start | bytes 8388608
  71.0 5.9 %slice-start.2 = ((s8[12582912]{0:T(1024)(128)(4,1)}), s8[4194304]{0:T(1024)(128)(4,1)S(1)}, s32[]{:S(2)}) async-start(s8[12582912]{0:T(1024)(128)(4,1)} %bitcast.146), calls=%async_computation.7 | async-start | bytes 8388608
  116.9 55.0 %all-to-all-start.3 = ((bf16[8,2,128,256]{3,2,1,0:T(8,128)(2,1)}), bf16[8,2,128,256]{3,2,1,0:T(8,128)(2,1)S(1)}, u32[]{:S(2)}, u32[]{:S(2)}) async-start(bf16[8,2,128,256]{3,2,1,0:T(8,128)(2,1)} %bitcast.39), calls=%async_computation.3 | async-start | bytes 2097152 | tf_op jit(solution)/shard_map/all_to_all | solution.py:125
  122.0 48.2 %copy-start.6 = (f32[16,128,128]{2,1,0:T(8,128)S(1)}, f32[16,128,128]{2,1,0:T(8,128)}, u32[]{:S(2)}) copy-start(f32[16,128,128]{2,1,0:T(8,128)} %fusion.100) | copy-start | bytes 3145732
  171.9 31.1 %all-to-all-start = ((f32[8,32,16,128]{3,2,1,0:T(8,128)}), f32[8,32,16,128]{3,2,1,0:T(8,128)S(1)}, u32[]{:S(2)}, u32[]{:S(2)}) async-start(f32[8,32,16,128]{3,2,1,0:T(8,128)} %bitcast.148), calls=%async_computation | async-start | bytes 4194304 | tf_op jit(solution)/shard_map/all_to_all | solution.py:27
  203.0 1.3 copy-start.5
  204.4 36.9 %all-to-all-start.4 = ((bf16[16,2,128,256]{3,1,2,0:T(2,128)(2,1)}), bf16[16,2,128,256]{3,1,2,0:T(2,128)(2,1)S(1)}, u32[]{:S(2)}, u32[]{:S(2)}) async-start(bf16[16,2,128,256]{3,1,2,0:T(2,128)(2,1)} %copy.129), calls=%async_computation.4 | async-start | bytes 4194304 | tf_op jit(solution)/shard_map/all_to_all | solution.py:161
  213.9 28.7 %copy-start.7 = (f32[2,256,256]{2,1,0:T(8,128)S(1)}, f32[2,256,256]{2,1,0:T(8,128)}, u32[]{:S(2)}) copy-start(f32[2,256,256]{2,1,0:T(8,128)} %param.19) | copy-start | bytes 1572868
  241.2 10.1 %copy-start.1 = (s32[16]{0:T(128)S(1)}, s32[16]{0:T(128)}, u32[]{:S(2)}) copy-start(s32[16]{0:T(128)} %param.18) | copy-start | bytes 196
where the time goes:
time: 253 us; the launch traced here: 251 us
  matrix products  146 us (58%)
  waiting for transfers between devices  42.5 us (17%)
  starting transfers between devices  35.9 us (14%)
  local copies, waits for them, and re-layouts  22.6 us (9%)
  other arithmetic  3.5 us (1%)
    dot_general x14, matrix products, shards(): jnp.einsum('crij,crjm->crim', masked, window, preferred_element_type=jnp....  69.7 us
    dot_general x1, matrix products, shards(): jnp.einsum('crbm,crbn->cmn', shaped, conducted, preferred_element_type=jn...  48.2 us
    all_to_all x1, waiting for transfers between devices, shards(): lax.all_to_all(packed.reshape(comp_size, own_cap, mode_count, port_block)...  27.4 us
    all_to_all x1, waiting for transfers between devices, sum_at_owner(): lax.all_to_all(pieces, axis, split_axis=0, concat_axis=0, tiled=True)  15.2 us
    reshape x2, local copies, waits for them, and re-layouts, shards(): packed.reshape(comp_size, own_cap, mode_count, port_block)  8.94 us
    dot_general x1, matrix products, shards(): jnp.einsum('nko,nkpq->kopq', weight, squares, precision=lax.Precision.HIG...  7.99 us
    dot_general x1, matrix products, shards(): jnp.einsum('crbm,crbn->cmn', shaped, weighted, preferred_element_type=jnp...  7.73 us
    all_to_all x1, starting transfers between devices, shards(): lax.all_to_all(packed.reshape(comp_size, own_cap, mode_count, port_block)...  6.91 us
  transfers between devices with their start and end apart: 7, of which 2 were waited for; matrix products, arithmetic and copies ran while one was open for 63% of the time, Pallas kernels for 0%

commit v1 on v0

v1 whole, which is shorter than its diff:
```python
import jax
import jax.numpy as jnp
from jax import lax
from jax.experimental import pallas as pl
from jax.experimental.pallas import tpu as pltpu
from jax.sharding import PartitionSpec as P

BF, F32, I32 = jnp.bfloat16, jnp.float32, jnp.int32
COMPS, PORTS = 16, 8
CD, NBL, NB, NP = 16, 8, 3, 4
BS, M, PB = 128, 128, 256
TOP = COMPS * 8


def nt(a, b):
    return lax.dot_general(a, b, (((1,), (1,)), ((), ())), preferred_element_type=F32)


def tn(a, b):
    return lax.dot_general(a, b, (((0,), (0,)), ((), ())), preferred_element_type=F32)


def remote(src, dst, send, recv, **where):
    return pltpu.make_async_remote_copy(
        src_ref=src,
        dst_ref=dst,
        send_sem=send,
        recv_sem=recv,
        device_id=where,
        device_id_type=pl.DeviceIdType.MESH,
    )


def fill_tables(me_port, ports_s, surface_s, ports_v, surface_v, counts_v, table):
    ports, surface = ports_v[...], surface_v[...]
    owner, target = (ports >> 1) & 7, ports >> 4
    shard = surface >> 3
    cell, device = shard * 8 + owner, ports >> 1
    comp = lax.broadcasted_iota(I32, (NP, CD), 1)
    slot = lax.broadcasted_iota(I32, (NP, CD), 0)
    order = comp * NP + slot
    alive = slot < counts_v[...]

    def count(c, ranks):
        in_cell, in_device = ranks
        for s in range(NP):
            port, block, at = ports_s[s, c], surface_s[s, c], c * NP + s
            this_device = port >> 1
            this_cell = (block >> 3) * 8 + (this_device & 7)
            later = order > at
            in_cell += jnp.where(later & (cell == this_cell), 1, 0)
            in_device += jnp.where(later & (device == this_device), 1, 0)
        return in_cell, in_device

    zero = jnp.zeros((NP, CD), I32)
    in_cell, in_device = lax.fori_loop(0, CD, count, (zero, zero))
    code = 2048 + (ports & 1) * 1024 + (shard * 2 + in_cell) * 64 + order
    here = alive & (owner == me_port)
    code = jnp.where(here, code, 0)
    device_key = target * 2 + in_device
    row = comp * NBL + (surface & 7)
    cell_key = jnp.where(shard == me_port, owner * 2 + in_cell, -1)
    q = lax.broadcasted_iota(I32, (TOP, CD), 0)
    wanted = (q >> 3) * 2 + (q & 1)
    total = jnp.zeros((TOP, CD), I32)
    for s in range(NP):
        total += jnp.where(device_key[s : s + 1] == wanted, code[s : s + 1], 0)
    table[0:TOP] = jnp.broadcast_to(jnp.sum(total, axis=1, keepdims=True), (TOP, 128))
    wanted = lax.broadcasted_iota(I32, (16, CD), 0)
    total = jnp.zeros((16, CD), I32)
    for s in range(NP):
        total += jnp.where(cell_key[s : s + 1] == wanted, row[s : s + 1], 0)
    table[TOP : TOP + 16] = jnp.broadcast_to(jnp.sum(total, axis=1, keepdims=True), (16, 128))


def kernel(
    offs,
    ports_s,
    surface_s,
    ports_v,
    surface_v,
    counts_v,
    shapes,
    values,
    cond_hbm,
    cap_hbm,
    coupling,
    boundary,
    cond_out,
    cap_out,
    face_out,
    phi,
    vals,
    coup,
    cond,
    cap,
    bound,
    table,
    table_s,
    codes,
    codes_s,
    rows_out,
    rows_in,
    halo_lo,
    halo_hi,
    win,
    scaled,
    part,
    pair_in,
    zsum,
    z_in,
    fac_out,
    fac_in,
    acc,
    load_sem,
    vals_sem,
    rows_ss,
    rows_rs,
    halo_ss,
    halo_rs,
    pair_ss,
    pair_rs,
    z_ss,
    z_rs,
    fac_ss,
    fac_rs,
    code_ss,
    code_rs,
):
    c_me, p_me = lax.axis_index("comp"), lax.axis_index("port")
    y, x = c_me // 4, c_me % 4
    z, core = p_me // 2, p_me % 2
    before, after = (p_me + PORTS - 1) % PORTS, (p_me + 1) % PORTS

    def to_comp(j):
        return ((y + j // 4) % 4) * 4 + (x + j % 4) % 4

    def from_comp(j):
        return ((y + 4 - j // 4) % 4) * 4 + (x + 4 - j % 4) % 4

    barrier = pltpu.get_barrier_semaphore()

    @pl.loop(1, PORTS)
    def _(j):
        pl.semaphore_signal(barrier, 1, device_id={"port": (p_me + j) % PORTS}, device_id_type=pl.DeviceIdType.MESH)

    @pl.loop(1, COMPS)
    def _(j):
        pl.semaphore_signal(barrier, 1, device_id={"comp": to_comp(j)}, device_id_type=pl.DeviceIdType.MESH)

    load_phi = pltpu.make_async_copy(shapes, phi, load_sem.at[0])
    load_coup = pltpu.make_async_copy(coupling, coup, load_sem.at[1])
    load_cond = pltpu.make_async_copy(cond_hbm, cond, load_sem.at[2])
    load_cap = pltpu.make_async_copy(cap_hbm, cap, load_sem.at[3])
    load_bound = pltpu.make_async_copy(boundary, bound, load_sem.at[4])
    load_phi.start()
    load_coup.start()
    load_cond.start()
    load_cap.start()

    def load_vals(c):
        return pltpu.make_async_copy(values.at[c], vals.at[c], vals_sem.at[c])

    @pl.loop(0, CD)
    def _(c):
        load_vals(c).start()

    load_bound.start()
    fill_tables(p_me, ports_s, surface_s, ports_v, surface_v, counts_v, table)
    to_smem = pltpu.make_async_copy(table, table_s, load_sem.at[5])
    to_smem.start()
    load_phi.wait()
    to_smem.wait()

    @pl.loop(0, PORTS)
    def _(o):
        for k in range(2):
            picked = table_s[TOP + 2 * o + k, 0]
            rows_out[o, k] = phi[picked].T

    rows_in[p_me] = rows_out[p_me]
    codes[pl.ds(pl.multiple_of(c_me * 8, 8), 8)] = table[pl.ds(pl.multiple_of(c_me * 8, 8), 8)]
    pl.semaphore_wait(barrier, PORTS - 1 + COMPS - 1)

    def send_rows(j):
        o = (p_me + j) % PORTS
        return remote(rows_out.at[o], rows_in.at[p_me], rows_ss.at[o], rows_rs.at[p_me], port=o)

    def recv_rows(j):
        o = (p_me + PORTS - j) % PORTS
        return remote(rows_out.at[o], rows_in.at[o], rows_ss.at[o], rows_rs.at[o], port=o)

    @pl.loop(1, PORTS)
    def _(j):
        send_rows(j).start()

    def send_up(c):
        return remote(
            shapes.at[pl.ds(c * NBL + NBL - 2, 2)], halo_lo.at[c], halo_ss.at[0, c], halo_rs.at[0, c], port=after
        )

    def send_down(c):
        return remote(shapes.at[pl.ds(c * NBL, 2)], halo_hi.at[c], halo_ss.at[1, c], halo_rs.at[1, c], port=before)

    @pl.loop(0, CD)
    def _(c):
        send_up(c).start()
        send_down(c).start()

    def send_codes(j):
        d = to_comp(j)
        return remote(
            table.at[pl.ds(pl.multiple_of(d * 8, 8), 8)],
            codes.at[pl.ds(pl.multiple_of(c_me * 8, 8), 8)],
            code_ss.at[d],
            code_rs.at[c_me],
            comp=d,
        )

    def recv_codes(j):
        d = from_comp(j)
        return remote(
            table.at[pl.ds(pl.multiple_of(d * 8, 8), 8)],
            codes.at[pl.ds(pl.multiple_of(d * 8, 8), 8)],
            code_ss.at[d],
            code_rs.at[d],
            comp=d,
        )

    @pl.loop(1, COMPS)
    def _(j):
        send_codes(j).start()

    load_coup.wait()

    @pl.loop(1, PORTS)
    def _(j):
        recv_rows(j).wait_recv()

    def factor(d, k):
        code = table_s[d * 8 + k, 0]
        rows = rows_in[(code >> 7) & 7, (code >> 6) & 1]
        return jnp.dot(rows, coup[code & 63], preferred_element_type=F32).astype(BF)

    def send_factors(j):
        d = to_comp(j)
        return remote(fac_out.at[d], fac_in.at[c_me], fac_ss.at[d], fac_rs.at[c_me], comp=d)

    def recv_factors(j):
        d = from_comp(j)
        return remote(fac_out.at[d], fac_in.at[d], fac_ss.at[d], fac_rs.at[d], comp=d)

    @pl.loop(1, COMPS)
    def _(j):
        d = to_comp(j)
        for k in range(2):
            fac_out[d, pl.ds(k * M, M)] = factor(d, k)
        send_factors(j).start()

    for k in range(2):
        fac_in[c_me, pl.ds(k * M, M)] = factor(c_me, k)

    def send_pair(c):
        return remote(
            part.at[1 - core, :, c], pair_in.at[:, c], pair_ss.at[c], pair_rs.at[c], port=2 * z + 1 - core
        )

    def send_z(d, h):
        to = (z + d) % 4
        return remote(
            zsum.at[to, pl.ds(2 * h, 2)], z_in.at[z, pl.ds(2 * h, 2)], z_ss.at[to, h], z_rs.at[z, h], port=2 * to + core
        )

    def recv_z(d, h):
        at = (z + 4 - d) % 4
        return remote(
            zsum.at[at, pl.ds(2 * h, 2)], z_in.at[at, pl.ds(2 * h, 2)], z_ss.at[at, h], z_rs.at[at, h], port=2 * at + core
        )

    def chip_sums(h):
        for i in range(2):
            c = 2 * h + i
            send_pair(c).wait_recv()
            zsum[:, c] = part[core, :, c] + pair_in[:, c]
        for d in range(1, 4):
            send_z(d, h).start()

    first = jnp.where(p_me == 0, 0.0, 1.0)
    last = jnp.where(p_me == PORTS - 1, 0.0, 1.0)

    def modal(c):
        load_vals(c).wait()
        send_up(c).wait_recv()
        send_down(c).wait_recv()
        for i in range(2):
            win[i] = (halo_lo[c, i].astype(F32) * first).T.astype(BF)
            win[NBL + 2 + i] = (halo_hi[c, i].astype(F32) * last).T.astype(BF)
        for r in range(NBL):
            win[2 + r] = phi[c * NBL + r].T
        base = pl.multiple_of((c // 8) * 8, 8)
        mine = lax.broadcasted_iota(I32, (8, NBL * BS), 0) == c % 8
        cond_row = jnp.sum(jnp.where(mine, cond[pl.ds(base, 8)], 0.0), axis=0, keepdims=True)
        cap_row = jnp.sum(jnp.where(mine, cap[pl.ds(base, 8)], 0.0), axis=0, keepdims=True)
        for r in range(NBL):
            cells = slice(r * BS, (r + 1) * BS)
            near = jnp.concatenate([win[r + 2 + offs[k, r, c]] for k in range(NB)], axis=1)
            blocks = jnp.concatenate([vals[c, r, k] for k in range(NB)], axis=1)
            own = win[r + 2].astype(F32)
            scaled[0:M, cells] = (nt(near, blocks) + cond_row[:, cells] * own).astype(BF)
            scaled[M : 2 * M, cells] = (cap_row[:, cells] * own).astype(BF)
        every = jnp.concatenate([win[r + 2] for r in range(NBL)], axis=1)
        sums = nt(every, scaled[...])
        for p in range(PORTS):
            part[p % 2, p // 2, c] = sums[16 * p : 16 * p + 16]

    load_cond.wait()
    load_cap.wait()

    @pl.loop(0, CD // 2)
    def _(h):
        @pl.loop(0, 2)
        def _(i):
            modal(2 * h + i)
            send_pair(2 * h + i).start()

        @pl.when(h > 0)
        def _():
            chip_sums(h - 1)

    chip_sums(CD // 2 - 1)

    @pl.loop(1, COMPS)
    def _(j):
        recv_codes(j).wait_recv()

    to_smem = pltpu.make_async_copy(codes, codes_s, load_sem.at[6])
    to_smem.start()
    acc[...] = jnp.zeros_like(acc)
    to_smem.wait()

    def square(d):
        for o in range(2):
            halves = []
            for k in range(2):
                code = codes_s[d * 8 + k, 0]
                weight = jnp.where((code >> 10) == 2 + o, 1.0, 0.0).astype(F32)
                halves.append((fac_in[d, pl.ds(k * M, M)].astype(F32) * weight).astype(BF))
            acc[o] += tn(jnp.concatenate(halves, axis=0), fac_in[d])

    square(c_me)

    @pl.loop(1, COMPS)
    def _(j):
        recv_factors(j).wait_recv()
        square(from_comp(j))

    load_bound.wait()
    face_out[...] = bound[...] + acc[...] * (1.0 / M)

    @pl.loop(0, CD // 2)
    def _(h):
        for d in range(1, 4):
            recv_z(d, h).wait_recv()
        for i in range(2):
            c = 2 * h + i
            total = zsum[z, c]
            for d in range(1, 4):
                total = total + z_in[(z + 4 - d) % 4, c]
            cond_out[c] = total[:, 0:M]
            cap_out[c] = total[:, M : 2 * M]
        for d in range(1, 4):
            send_z(d, h).wait_send()

    @pl.loop(0, CD)
    def _(c):
        send_up(c).wait_send()
        send_down(c).wait_send()
        send_pair(c).wait_send()

    @pl.loop(1, PORTS)
    def _(j):
        send_rows(j).wait_send()

    @pl.loop(1, COMPS)
    def _(j):
        send_factors(j).wait_send()
        send_codes(j).wait_send()


def shards(
    mode_shapes,
    block_values,
    block_offsets,
    conductance,
    capacity,
    coupling,
    surface_blocks,
    port_ids,
    port_counts,
    boundary,
):
    smem = pl.BlockSpec(memory_space=pltpu.SMEM)
    vmem = pl.BlockSpec(memory_space=pltpu.VMEM)
    hbm = pl.BlockSpec(memory_space=pl.ANY)
    dma = pltpu.SemaphoreType.DMA
    ports, surface = port_ids.T, surface_blocks.T
    return pl.pallas_call(
        kernel,
        out_shape=(
            jax.ShapeDtypeStruct((CD, M // PORTS, M), F32),
            jax.ShapeDtypeStruct((CD, M // PORTS, M), F32),
            jax.ShapeDtypeStruct((2, PB, PB), F32),
        ),
        in_specs=[smem] * 3 + [vmem] * 3 + [hbm] * 6,
        out_specs=(vmem, vmem, vmem),
        scratch_shapes=[
            pltpu.VMEM((CD * NBL, BS, M), BF),
            pltpu.VMEM((CD, NBL, NB, BS, BS), BF),
            pltpu.VMEM((CD * NP, BS, PB), BF),
            pltpu.VMEM((CD, NBL * BS), F32),
            pltpu.VMEM((CD, NBL * BS), F32),
            pltpu.VMEM((2, PB, PB), F32),
            pltpu.VMEM((TOP + 16, 128), I32),
            pltpu.SMEM((TOP + 16, 128), I32),
            pltpu.VMEM((TOP, 128), I32),
            pltpu.SMEM((TOP, 128), I32),
            pltpu.VMEM((PORTS, 2, M, BS), BF),
            pltpu.VMEM((PORTS, 2, M, BS), BF),
            pltpu.VMEM((CD, 2, BS, M), BF),
            pltpu.VMEM((CD, 2, BS, M), BF),
            pltpu.VMEM((NBL + 4, M, BS), BF),
            pltpu.VMEM((2 * M, NBL * BS), BF),
            pltpu.VMEM((2, 4, CD, 16, 2 * M), F32),
            pltpu.VMEM((4, CD, 16, 2 * M), F32),
            pltpu.VMEM((4, CD, 16, 2 * M), F32),
            pltpu.VMEM((4, CD, 16, 2 * M), F32),
            pltpu.VMEM((COMPS, 2 * M, PB), BF),
            pltpu.VMEM((COMPS, 2 * M, PB), BF),
            pltpu.VMEM((2, PB, PB), F32),
            dma((7,)),
            dma((CD,)),
            dma((PORTS,)),
            dma((PORTS,)),
            dma((2, CD)),
            dma((2, CD)),
            dma((CD,)),
            dma((CD,)),
            dma((4, CD // 2)),
            dma((4, CD // 2)),
            dma((COMPS,)),
            dma((COMPS,)),
            dma((COMPS,)),
            dma((COMPS,)),
        ],
        compiler_params=pltpu.CompilerParams(
            collective_id=0, has_side_effects=True, vmem_limit_bytes=60 << 20
        ),
        name="reduce_components",
    )(
        block_offsets.transpose(2, 1, 0),
        ports,
        surface,
        ports,
        surface,
        port_counts.reshape(1, CD),
        mode_shapes.reshape(CD * NBL, BS, M),
        block_values,
        conductance,
        capacity,
        coupling.reshape(CD * NP, BS, PB),
        boundary,
    )


def solution(mesh):
    in_specs = (
        P("comp", "port", None),
        P("comp", "port", None, None, None),
        P("comp", "port", None),
        P("comp", "port"),
        P("comp", "port"),
        P("comp", None, None, None),
        P("comp", None),
        P("comp", None),
        P("comp"),
        P(("comp", "port"), None, None),
    )
    out_specs = (P("comp", "port", None), P("comp", "port", None), P(("comp", "port"), None, None))
    return jax.shard_map(shards, mesh=mesh, in_specs=in_specs, out_specs=out_specs, check_vma=False)
```

time: 253 us -> 60.6 us (0.24)
  matrix products: 146 us -> 0 us
  Pallas kernels: 0 us -> 54.7 us
  waiting for transfers between devices: 42.5 us -> 0 us
  starting transfers between devices: 35.9 us -> 0 us
  local copies, waits for them, and re-layouts: 22.6 us -> 5 us
  other arithmetic: 3.5 us -> 0 us
    dot_general x22 -> x0, matrix products: 146 us -> none  [the longest x14 69.7 us: shards(): jnp.einsum('crij,crjm->crim', masked, window, preferred_element_type=jnp....]
    pallas_call x0 -> x1, Pallas kernels: none -> 54.7 us  [shards(): pl.pallas_call(kernel, out_shape=(jax.ShapeDtypeStruct((CD, M // PORTS, M...]
    all_to_all x5 -> x0, waiting for transfers between devices: 42.5 us -> none  [the longest x1 27.4 us: shards(): lax.all_to_all(packed.reshape(comp_size, own_cap, mode_count, port_block)...]
    all_to_all x5 -> x0, starting transfers between devices: 29.1 us -> none  [the longest x1 6.91 us: shards(): lax.all_to_all(packed.reshape(comp_size, own_cap, mode_count, port_block)...]
    reshape x6 -> x0, local copies, waits for them, and re-layouts: 10.7 us -> none  [the longest x2 8.94 us: shards(): packed.reshape(comp_size, own_cap, mode_count, port_block)]
    ppermute x2 -> x0, starting transfers between devices: 6.84 us -> none  [the longest x1 4.92 us: padded_2(): before = lax.ppermute(last, axis, up)]
    gather x4 -> x0, local copies, waits for them, and re-layouts: 2.74 us -> none  [the longest x2 1.31 us: shards(): target = comp_of[source] * block_rows + surface_flat[source] % block_rows]
    slice x1 -> x0, local copies, waits for them, and re-layouts: 2.72 us -> none  [padded_2(): last = lax.slice_in_dim(value, length - width, length, axis=dim)]
  transfers between devices with their start and end apart: 7 -> 0, of which waited for: 2 -> 0; matrix products, arithmetic and copies ran while one was open for 63% -> 0% of each run, Pallas kernels for 0% -> 0%
where the time goes in v1:
time: 60.6 us; the launch traced here: 60.4 us
  Pallas kernels  54.7 us (90%)
  local copies, waits for them, and re-layouts  5 us (8%)
  between operations  0.64 us (1%)
    pallas_call x1, Pallas kernels, shards(): pl.pallas_call(kernel, out_shape=(jax.ShapeDtypeStruct((CD, M // PORTS, M...  54.7 us
    unnamed x3, local copies, waits for them, and re-layouts  5 us

profile of v1, /device:TPU:1, one launch (start us, length us, event | category | flops | bytes accessed | tf_op | source)
XLA Modules:
  0.0 60.4 jit_solution(7894188437851868704)
XLA Ops:
  0.6 54.7 %reduce_components.1 = (f32[16,16,128]{2,1,0:T(8,128)}, f32[16,16,128]{2,1,0:T(8,128)}, f32[2,256,256]{2,1,0:T(8,128)}) custom-call(s32[3,8,16]{2,1,0:T(8,128)} %bitcast.8, s32[4,16]{1,0:T(4,128)} %bitcast.9, s32[4,16]{1,0:T(4,128)} %bitcast.11, s32[4,16]{1,0:T(4,128)} %bitcast.10, s32[4,16]{1,0:T(4,128)} %bitcast.12, s32[1,16]{1,0:T(1,128)} %bitcast.13, ...), custom_call_target="tpu_custom_call" | custom-call | tf_op jit(solution)/shard_map/reduce_components/pallas_call | solution.py:407
  55.3 1.6 %copy.16 = f32[16,16,128]{2,1,0:T(8,128)} copy(f32[16,16,128]{2,1,0:T(8,128)} %get-tuple-element.6) | data formatting | bytes 262144
  56.9 1.6 %copy.17 = f32[16,16,128]{2,1,0:T(8,128)} copy(f32[16,16,128]{2,1,0:T(8,128)} %get-tuple-element.7) | data formatting | bytes 262144
  58.5 1.9 %copy.18 = f32[2,256,256]{2,1,0:T(8,128)} copy(f32[2,256,256]{2,1,0:T(8,128)} %get-tuple-element.8) | data formatting | bytes 1048576

commit v2 on v1

--- a/solution.py
+++ b/solution.py
@@ -9,6 +9,9 @@
 COMPS, PORTS = 16, 8
 CD, NBL, NB, NP = 16, 8, 3, 4
 BS, M, PB = 128, 128, 256
+HOPS = ((0, 1), (0, 3), (1, 0), (3, 0), (1, 1), (3, 3), (1, 3), (3, 1), (2, 0), (0, 2), (2, 3), (2, 1), (3, 2), (1, 2), (2, 2))
+EARLY = 8
+Z_HOPS = (4, 5, 2, 3, 6, 7, 1)
 TOP = COMPS * 8
 
 
@@ -86,8 +89,7 @@
     cap_hbm,
     coupling,
     boundary,
-    cond_out,
-    cap_out,
+    sums_out,
     face_out,
     phi,
     vals,
@@ -111,6 +113,9 @@
     z_in,
     fac_out,
     fac_in,
+    late_out,
+    late_in,
+    both,
     acc,
     load_sem,
     vals_sem,
@@ -126,17 +131,19 @@
     fac_rs,
     code_ss,
     code_rs,
+    late_ss,
+    late_rs,
 ):
     c_me, p_me = lax.axis_index("comp"), lax.axis_index("port")
     y, x = c_me // 4, c_me % 4
     z, core = p_me // 2, p_me % 2
     before, after = (p_me + PORTS - 1) % PORTS, (p_me + 1) % PORTS
 
-    def to_comp(j):
-        return ((y + j // 4) % 4) * 4 + (x + j % 4) % 4
-
-    def from_comp(j):
-        return ((y + 4 - j // 4) % 4) * 4 + (x + 4 - j % 4) % 4
+    def to_comp(hop):
+        return ((y + hop[0]) % 4) * 4 + (x + hop[1]) % 4
+
+    def from_comp(hop):
+        return ((y + 4 - hop[0]) % 4) * 4 + (x + 4 - hop[1]) % 4
 
     barrier = pltpu.get_barrier_semaphore()
 
@@ -144,9 +151,8 @@
     def _(j):
         pl.semaphore_signal(barrier, 1, device_id={"port": (p_me + j) % PORTS}, device_id_type=pl.DeviceIdType.MESH)
 
-    @pl.loop(1, COMPS)
-    def _(j):
-        pl.semaphore_signal(barrier, 1, device_id={"comp": to_comp(j)}, device_id_type=pl.DeviceIdType.MESH)
+    for hop in HOPS:
+        pl.semaphore_signal(barrier, 1, device_id={"comp": to_comp(hop)}, device_id_type=pl.DeviceIdType.MESH)
 
     load_phi = pltpu.make_async_copy(shapes, phi, load_sem.at[0])
     load_coup = pltpu.make_async_copy(coupling, coup, load_sem.at[1])
@@ -190,8 +196,7 @@
         o = (p_me + PORTS - j) % PORTS
         return remote(rows_out.at[o], rows_in.at[o], rows_ss.at[o], rows_rs.at[o], port=o)
 
-    @pl.loop(1, PORTS)
-    def _(j):
+    for j in Z_HOPS:
         send_rows(j).start()
 
     def send_up(c):
@@ -207,8 +212,8 @@
         send_up(c).start()
         send_down(c).start()
 
-    def send_codes(j):
-        d = to_comp(j)
+    def send_codes(hop):
+        d = to_comp(hop)
         return remote(
             table.at[pl.ds(pl.multiple_of(d * 8, 8), 8)],
             codes.at[pl.ds(pl.multiple_of(c_me * 8, 8), 8)],
@@ -217,8 +222,8 @@
             comp=d,
         )
 
-    def recv_codes(j):
-        d = from_comp(j)
+    def recv_codes(hop):
+        d = from_comp(hop)
         return remote(
             table.at[pl.ds(pl.multiple_of(d * 8, 8), 8)],
             codes.at[pl.ds(pl.multiple_of(d * 8, 8), 8)],
@@ -227,35 +232,53 @@
             comp=d,
         )
 
-    @pl.loop(1, COMPS)
-    def _(j):
-        send_codes(j).start()
+    def send_factors(hop):
+        d = to_comp(hop)
+        return remote(fac_out.at[d], fac_in.at[c_me], fac_ss.at[d], fac_rs.at[c_me], comp=d)
+
+    def recv_factors(hop):
+        d = from_comp(hop)
+        return remote(fac_out.at[d], fac_in.at[d], fac_ss.at[d], fac_rs.at[d], comp=d)
+
+    def send_late(hop):
+        d = to_comp(hop)
+        return remote(late_out.at[d], late_in.at[c_me], late_ss.at[d], late_rs.at[c_me], comp=d)
+
+    def recv_late(hop):
+        d = from_comp(hop)
+        return remote(late_out.at[d], late_in.at[d], late_ss.at[d], late_rs.at[d], comp=d)
 
     load_coup.wait()
+    for hop in HOPS[:EARLY]:
+        d = to_comp(hop)
+        for k in range(2):
+            fac_out[d, pl.ds(k * M, M)] = coup[table_s[d * 8 + k, 0] & 63]
+        send_factors(hop).start()
+
+    for hop in HOPS:
+        send_codes(hop).start()
 
     @pl.loop(1, PORTS)
     def _(j):
         recv_rows(j).wait_recv()
 
+    def row_of(code):
+        return rows_in[(code >> 7) & 7, (code >> 6) & 1]
+
     def factor(d, k):
         code = table_s[d * 8 + k, 0]
-        rows = rows_in[(code >> 7) & 7, (code >> 6) & 1]
-        return jnp.dot(rows, coup[code & 63], preferred_element_type=F32).astype(BF)
-
-    def send_factors(j):
-        d = to_comp(j)
-        return remote(fac_out.at[d], fac_in.at[c_me], fac_ss.at[d], fac_rs.at[c_me], comp=d)
-
-    def recv_factors(j):
-        d = from_comp(j)
-        return remote(fac_out.at[d], fac_in.at[d], fac_ss.at[d], fac_rs.at[d], comp=d)
-
-    @pl.loop(1, COMPS)
-    def _(j):
-        d = to_comp(j)
+        return jnp.dot(row_of(code), coup[code & 63], preferred_element_type=F32).astype(BF)
+
+    for hop in HOPS[:EARLY]:
+        d = to_comp(hop)
+        for k in range(2):
+            late_out[d, k] = row_of(table_s[d * 8 + k, 0])
+        send_late(hop).start()
+    for hop in HOPS[EARLY:]:
+        d = to_comp(hop)
         for k in range(2):
             fac_out[d, pl.ds(k * M, M)] = factor(d, k)
-        send_factors(j).start()
+        send_factors(hop).start()
 
     for k in range(2):
         fac_in[c_me, pl.ds(k * M, M)] = factor(c_me, k)
@@ -329,30 +352,34 @@
 
     chip_sums(CD // 2 - 1)
 
-    @pl.loop(1, COMPS)
-    def _(j):
-        recv_codes(j).wait_recv()
-
+    for hop in HOPS:
+        recv_codes(hop).wait_recv()
     to_smem = pltpu.make_async_copy(codes, codes_s, load_sem.at[6])
     to_smem.start()
     acc[...] = jnp.zeros_like(acc)
     to_smem.wait()
 
-    def square(d):
+    def square(d, factors):
         for o in range(2):
             halves = []
             for k in range(2):
                 code = codes_s[d * 8 + k, 0]
                 weight = jnp.where((code >> 10) == 2 + o, 1.0, 0.0).astype(F32)
-                halves.append((fac_in[d, pl.ds(k * M, M)].astype(F32) * weight).astype(BF))
-            acc[o] += tn(jnp.concatenate(halves, axis=0), fac_in[d])
-
-    square(c_me)
-
-    @pl.loop(1, COMPS)
-    def _(j):
-        recv_factors(j).wait_recv()
-        square(from_comp(j))
+                halves.append((factors[pl.ds(k * M, M)].astype(F32) * weight).astype(BF))
+            acc[o] += tn(jnp.concatenate(halves, axis=0), factors[...])
+
+    square(c_me, fac_in.at[c_me])
+    for hop in HOPS[:EARLY]:
+        d = from_comp(hop)
+        recv_factors(hop).wait_recv()
+        recv_late(hop).wait_recv()
+        for k in range(2):
+            half = pl.ds(k * M, M)
+            both[half] = jnp.dot(late_in[d, k], fac_in[d, half], preferred_element_type=F32).astype(BF)
+        square(d, both)
+    for hop in HOPS[EARLY:]:
+        recv_factors(hop).wait_recv()
+        square(from_comp(hop), fac_in.at[from_comp(hop)])
 
     load_bound.wait()
     face_out[...] = bound[...] + acc[...] * (1.0 / M)
@@ -366,8 +393,7 @@
             total = zsum[z, c]
             for d in range(1, 4):
                 total = total + z_in[(z + 4 - d) % 4, c]
-            cond_out[c] = total[:, 0:M]
-            cap_out[c] = total[:, M : 2 * M]
+            sums_out[c] = total
         for d in range(1, 4):
             send_z(d, h).wait_send()
 
@@ -381,10 +407,17 @@
     def _(j):
         send_rows(j).wait_send()
 
-    @pl.loop(1, COMPS)
-    def _(j):
-        send_factors(j).wait_send()
-        send_codes(j).wait_send()
+    for hop in HOPS:
+        send_factors(hop).wait_send()
+        send_codes(hop).wait_send()
+    for hop in HOPS[:EARLY]:
+        send_late(hop).wait_send()
+
+
+def finish(sums, face, cond_out, cap_out, face_out):
+    cond_out[...] = sums[:, :, 0:M]
+    cap_out[...] = sums[:, :, M : 2 * M]
+    face_out[...] = face[...]
 
 
 def shards(
@@ -401,18 +434,18 @@
 ):
     smem = pl.BlockSpec(memory_space=pltpu.SMEM)
     vmem = pl.BlockSpec(memory_space=pltpu.VMEM)
-    hbm = pl.BlockSpec(memory_space=pl.ANY)
+    hbm = pl.BlockSpec(memory_space=pltpu.HBM)
     dma = pltpu.SemaphoreType.DMA
     ports, surface = port_ids.T, surface_blocks.T
-    return pl.pallas_call(
+    modal = jax.ShapeDtypeStruct((CD, M // PORTS, M), F32)
+    sums, face = pl.pallas_call(
         kernel,
         out_shape=(
-            jax.ShapeDtypeStruct((CD, M // PORTS, M), F32),
-            jax.ShapeDtypeStruct((CD, M // PORTS, M), F32),
+            jax.ShapeDtypeStruct((CD, M // PORTS, 2 * M), F32),
             jax.ShapeDtypeStruct((2, PB, PB), F32),
         ),
         in_specs=[smem] * 3 + [vmem] * 3 + [hbm] * 6,
-        out_specs=(vmem, vmem, vmem),
+        out_specs=(vmem, vmem),
         scratch_shapes=[
             pltpu.VMEM((CD * NBL, BS, M), BF),
             pltpu.VMEM((CD, NBL, NB, BS, BS), BF),
@@ -436,6 +469,9 @@
             pltpu.VMEM((4, CD, 16, 2 * M), F32),
             pltpu.VMEM((COMPS, 2 * M, PB), BF),
             pltpu.VMEM((COMPS, 2 * M, PB), BF),
+            pltpu.VMEM((COMPS, 2, M, BS), BF),
+            pltpu.VMEM((COMPS, 2, M, BS), BF),
+            pltpu.VMEM((2 * M, PB), BF),
             pltpu.VMEM((2, PB, PB), F32),
             dma((7,)),
             dma((CD,)),
@@ -451,9 +487,11 @@
             dma((COMPS,)),
             dma((COMPS,)),
             dma((COMPS,)),
+            dma((COMPS,)),
+            dma((COMPS,)),
         ],
         compiler_params=pltpu.CompilerParams(
-            collective_id=0, has_side_effects=True, vmem_limit_bytes=60 << 20
+            collective_id=0, has_side_effects=True, vmem_limit_bytes=63 << 20
         ),
         name="reduce_components",
     )(
@@ -470,6 +508,14 @@
         coupling.reshape(CD * NP, BS, PB),
         boundary,
     )
+    return pl.pallas_call(
+        finish,
+        out_shape=(modal, modal, jax.ShapeDtypeStruct((2, PB, PB), F32)),
+        in_specs=[vmem, vmem],
+        out_specs=(vmem, vmem, vmem),
+        compiler_params=pltpu.CompilerParams(vmem_limit_bytes=63 << 20),
+        name="finish",
+    )(sums, face)
 
 
 def solution(mesh):

time: 60.6 us -> 50.2 us (0.83)
  Pallas kernels: 54.7 us -> 49.3 us
  local copies, waits for them, and re-layouts: 5 us -> 0 us
    pallas_call x1 -> x2, Pallas kernels: 54.7 us -> 49.3 us  [the longest x1 47.3 us: shards(): pl.pallas_call(kernel, out_shape=(jax.ShapeDtypeStruct((CD, M // PORTS, 2...]
    unnamed x3 -> x0, local copies, waits for them, and re-layouts: 5 us -> none
where the time goes in v2:
time: 50.2 us; the launch traced here: 50 us
  Pallas kernels  49.3 us (98%)
  between operations  0.64 us (1%)
    pallas_call x1, Pallas kernels, shards(): pl.pallas_call(kernel, out_shape=(jax.ShapeDtypeStruct((CD, M // PORTS, 2...  47.3 us
    pallas_call x1, Pallas kernels, shards(): pl.pallas_call(finish, out_shape=(modal, modal, jax.ShapeDtypeStruct((2,...  2.01 us

profile of v2, /device:TPU:1, one launch (start us, length us, event | category | flops | bytes accessed | tf_op | source)
XLA Modules:
  0.0 50.0 jit_solution(12970778777623129180)
XLA Ops:
  0.6 47.3 %reduce_components.1 = (f32[16,16,256]{2,1,0:T(8,128)}, f32[2,256,256]{2,1,0:T(8,128)}) custom-call(s32[3,8,16]{2,1,0:T(8,128)} %bitcast.8, s32[4,16]{1,0:T(4,128)} %bitcast.9, s32[4,16]{1,0:T(4,128)} %bitcast.11, s32[4,16]{1,0:T(4,128)} %bitcast.10, s32[4,16]{1,0:T(4,128)} %bitcast.12, s32[1,16]{1,0:T(1,128)} %bitcast.13, bf16[128,128,128]{2,1,0:T(8,128)(2,1)} %bitcast.6, ...), custom_call_target="tpu_custom_call" | custom-call | tf_op jit(solution)/shard_map/reduce_components/pallas_call | solution.py:441
  48.0 2.0 %finish.1 = (f32[16,16,128]{2,1,0:T(8,128)}, f32[16,16,128]{2,1,0:T(8,128)}, f32[2,256,256]{2,1,0:T(8,128)}) custom-call(f32[16,16,256]{2,1,0:T(8,128)} %get-tuple-element.5.sums, f32[2,256,256]{2,1,0:T(8,128)} %get-tuple-element.6.face), custom_call_target="tpu_custom_call" | custom-call | tf_op jit(solution)/shard_map/finish/pallas_call | solution.py:511

commit v3 on v2

--- a/solution.py
+++ b/solution.py
@@ -11,6 +11,8 @@
 BS, M, PB = 128, 128, 256
 HOPS = ((0, 1), (0, 3), (1, 0), (3, 0), (1, 1), (3, 3), (1, 3), (3, 1), (2, 0), (0, 2), (2, 3), (2, 1), (3, 2), (1, 2), (2, 2))
 EARLY = 8
+LAST = 3
+AHEAD = 12
 Z_HOPS = (4, 5, 2, 3, 6, 7, 1)
 TOP = COMPS * 8
 
@@ -92,6 +94,7 @@
     sums_out,
     face_out,
     phi,
+    phi_t,
     vals,
     coup,
     cond,
@@ -184,6 +187,12 @@
             picked = table_s[TOP + 2 * o + k, 0]
             rows_out[o, k] = phi[picked].T
 
+    load_coup.wait()
+    for hop in HOPS[:EARLY]:
+        d = to_comp(hop)
+        for k in range(2):
+            fac_out[d, pl.ds(k * M, M)] = coup[table_s[d * 8 + k, 0] & 63]
+
     rows_in[p_me] = rows_out[p_me]
     codes[pl.ds(pl.multiple_of(c_me * 8, 8), 8)] = table[pl.ds(pl.multiple_of(c_me * 8, 8), 8)]
     pl.semaphore_wait(barrier, PORTS - 1 + COMPS - 1)
@@ -198,19 +207,6 @@
 
     for j in Z_HOPS:
         send_rows(j).start()
-
-    def send_up(c):
-        return remote(
-            shapes.at[pl.ds(c * NBL + NBL - 2, 2)], halo_lo.at[c], halo_ss.at[0, c], halo_rs.at[0, c], port=after
-        )
-
-    def send_down(c):
-        return remote(shapes.at[pl.ds(c * NBL, 2)], halo_hi.at[c], halo_ss.at[1, c], halo_rs.at[1, c], port=before)
-
-    @pl.loop(0, CD)
-    def _(c):
-        send_up(c).start()
-        send_down(c).start()
 
     def send_codes(hop):
         d = to_comp(hop)
@@ -248,15 +244,48 @@
         d = from_comp(hop)
         return remote(late_out.at[d], late_in.at[d], late_ss.at[d], late_rs.at[d], comp=d)
 
-    load_coup.wait()
     for hop in HOPS[:EARLY]:
-        d = to_comp(hop)
-        for k in range(2):
-            fac_out[d, pl.ds(k * M, M)] = coup[table_s[d * 8 + k, 0] & 63]
         send_factors(hop).start()
-
     for hop in HOPS:
         send_codes(hop).start()
+
+    def send_up(c):
+        return remote(
+            shapes.at[pl.ds(c * NBL + NBL - 2, 2)], halo_lo.at[c], halo_ss.at[0, c], halo_rs.at[0, c], port=after
+        )
+
+    def send_down(c):
+        return remote(shapes.at[pl.ds(c * NBL, 2)], halo_hi.at[c], halo_ss.at[1, c], halo_rs.at[1, c], port=before)
+
+    @pl.loop(0, CD)
+    def _(c):
+        send_up(c).start()
+        send_down(c).start()
+
+    def inner(c):
+        load_vals(c).wait()
+        for r in range(NBL):
+            phi_t[c * NBL + r] = phi[c * NBL + r].T
+        cond_row, cap_row = row_of_cells(cond, c), row_of_cells(cap, c)
+        for r in range(NBL):
+            cells = slice(r * BS, (r + 1) * BS)
+            own = phi_t[c * NBL + r].astype(F32)
+            scaled[c, M : 2 * M, cells] = (cap_row[:, cells] * own).astype(BF)
+            if 2 <= r < NBL - 2:
+                near = jnp.concatenate([phi_t[c * NBL + r + offs[k, r, c]] for k in range(NB)], axis=1)
+                scaled[c, 0:M, cells] = block_row(c, r, near, own, cond_row)
+
+    def row_of_cells(source, c):
+        mine = lax.broadcasted_iota(I32, (8, NBL * BS), 0) == c % 8
+        return jnp.sum(jnp.where(mine, source[pl.ds(pl.multiple_of((c // 8) * 8, 8), 8)], 0.0), axis=0, keepdims=True)
+
+    def block_row(c, r, near, own, cond_row):
+        blocks = jnp.concatenate([vals[c, r, k] for k in range(NB)], axis=1)
+        return (nt(near, blocks) + cond_row[:, r * BS : (r + 1) * BS] * own).astype(BF)
+
+    load_cond.wait()
+    load_cap.wait()
+    pl.loop(0, AHEAD)(inner)
 
     @pl.loop(1, PORTS)
     def _(j):
@@ -312,32 +341,23 @@
     last = jnp.where(p_me == PORTS - 1, 0.0, 1.0)
 
     def modal(c):
-        load_vals(c).wait()
         send_up(c).wait_recv()
         send_down(c).wait_recv()
         for i in range(2):
             win[i] = (halo_lo[c, i].astype(F32) * first).T.astype(BF)
             win[NBL + 2 + i] = (halo_hi[c, i].astype(F32) * last).T.astype(BF)
         for r in range(NBL):
-            win[2 + r] = phi[c * NBL + r].T
-        base = pl.multiple_of((c // 8) * 8, 8)
-        mine = lax.broadcasted_iota(I32, (8, NBL * BS), 0) == c % 8
-        cond_row = jnp.sum(jnp.where(mine, cond[pl.ds(base, 8)], 0.0), axis=0, keepdims=True)
-        cap_row = jnp.sum(jnp.where(mine, cap[pl.ds(base, 8)], 0.0), axis=0, keepdims=True)
-        for r in range(NBL):
-            cells = slice(r * BS, (r + 1) * BS)
+            win[2 + r] = phi_t[c * NBL + r]
+        cond_row = row_of_cells(cond, c)
+        for r in (0, 1, NBL - 2, NBL - 1):
             near = jnp.concatenate([win[r + 2 + offs[k, r, c]] for k in range(NB)], axis=1)
-            blocks = jnp.concatenate([vals[c, r, k] for k in range(NB)], axis=1)
-            own = win[r + 2].astype(F32)
-            scaled[0:M, cells] = (nt(near, blocks) + cond_row[:, cells] * own).astype(BF)
-            scaled[M : 2 * M, cells] = (cap_row[:, cells] * own).astype(BF)
-        every = jnp.concatenate([win[r + 2] for r in range(NBL)], axis=1)
-        sums = nt(every, scaled[...])
+            scaled[c, 0:M, r * BS : (r + 1) * BS] = block_row(c, r, near, win[r + 2].astype(F32), cond_row)
+        every = jnp.concatenate([phi_t[c * NBL + r] for r in range(NBL)], axis=1)
+        sums = nt(every, scaled[c])
         for p in range(PORTS):
             part[p % 2, p // 2, c] = sums[16 * p : 16 * p + 16]
 
-    load_cond.wait()
-    load_cap.wait()
+    pl.loop(AHEAD, CD)(inner)
 
     @pl.loop(0, CD // 2)
     def _(h):
@@ -351,6 +371,20 @@
             chip_sums(h - 1)
 
     chip_sums(CD // 2 - 1)
+
+    def gather_sums():
+        @pl.loop(0, CD // 2)
+        def _(h):
+            for d in range(1, 4):
+                recv_z(d, h).wait_recv()
+            for i in range(2):
+                c = 2 * h + i
+                total = zsum[z, c]
+                for d in range(1, 4):
+                    total = total + z_in[(z + 4 - d) % 4, c]
+                sums_out[c] = total
+            for d in range(1, 4):
+                send_z(d, h).wait_send()
 
     for hop in HOPS:
         recv_codes(hop).wait_recv()
@@ -377,25 +411,14 @@
             half = pl.ds(k * M, M)
             both[half] = jnp.dot(late_in[d, k], fac_in[d, half], preferred_element_type=F32).astype(BF)
         square(d, both)
-    for hop in HOPS[EARLY:]:
+    for at, hop in enumerate(HOPS[EARLY:]):
+        if at == len(HOPS) - EARLY - LAST:
+            gather_sums()
         recv_factors(hop).wait_recv()
         square(from_comp(hop), fac_in.at[from_comp(hop)])
 
     load_bound.wait()
     face_out[...] = bound[...] + acc[...] * (1.0 / M)
-
-    @pl.loop(0, CD // 2)
-    def _(h):
-        for d in range(1, 4):
-            recv_z(d, h).wait_recv()
-        for i in range(2):
-            c = 2 * h + i
-            total = zsum[z, c]
-            for d in range(1, 4):
-                total = total + z_in[(z + 4 - d) % 4, c]
-            sums_out[c] = total
-        for d in range(1, 4):
-            send_z(d, h).wait_send()
 
     @pl.loop(0, CD)
     def _(c):
@@ -441,13 +464,14 @@
     sums, face = pl.pallas_call(
         kernel,
         out_shape=(
-            jax.ShapeDtypeStruct((CD, M // PORTS, 2 * M), F32),
-            jax.ShapeDtypeStruct((2, PB, PB), F32),
+            pltpu.VMEM((CD, M // PORTS, 2 * M), F32),
+            pltpu.VMEM((2, PB, PB), F32),
         ),
         in_specs=[smem] * 3 + [vmem] * 3 + [hbm] * 6,
         out_specs=(vmem, vmem),
         scratch_shapes=[
             pltpu.VMEM((CD * NBL, BS, M), BF),
+            pltpu.VMEM((CD * NBL, M, BS), BF),
             pltpu.VMEM((CD, NBL, NB, BS, BS), BF),
             pltpu.VMEM((CD * NP, BS, PB), BF),
             pltpu.VMEM((CD, NBL * BS), F32),
@@ -462,7 +486,7 @@
             pltpu.VMEM((CD, 2, BS, M), BF),
             pltpu.VMEM((CD, 2, BS, M), BF),
             pltpu.VMEM((NBL + 4, M, BS), BF),
-            pltpu.VMEM((2 * M, NBL * BS), BF),
+            pltpu.VMEM((CD, 2 * M, NBL * BS), BF),
             pltpu.VMEM((2, 4, CD, 16, 2 * M), F32),
             pltpu.VMEM((4, CD, 16, 2 * M), F32),
             pltpu.VMEM((4, CD, 16, 2 * M), F32),
@@ -491,7 +515,7 @@
             dma((COMPS,)),
         ],
         compiler_params=pltpu.CompilerParams(
-            collective_id=0, has_side_effects=True, vmem_limit_bytes=63 << 20
+            collective_id=0, has_side_effects=True, vmem_limit_bytes=62 << 20
         ),
         name="reduce_components",
     )(
@@ -513,9 +537,9 @@
         out_shape=(modal, modal, jax.ShapeDtypeStruct((2, PB, PB), F32)),
         in_specs=[vmem, vmem],
         out_specs=(vmem, vmem, vmem),
-        compiler_params=pltpu.CompilerParams(vmem_limit_bytes=63 << 20),
+        compiler_params=pltpu.CompilerParams(vmem_limit_bytes=62 << 20),
         name="finish",
-    )(sums, face)
+    )(pltpu.with_memory_space_constraint(sums, pltpu.VMEM), pltpu.with_memory_space_constraint(face, pltpu.VMEM))
 
 
 def solution(mesh):

time: 50.2 us -> 48.1 us (0.958)
  Pallas kernels: 49.3 us -> 47.3 us
    pallas_call x1, Pallas kernels: 2.01 us -> 0.93 us  [shards(): pl.pallas_call(finish, out_shape=(modal, modal, jax.ShapeDtypeStruct((2,...]
    pallas_call x1, Pallas kernels: 47.3 us -> 46.4 us  [shards(): pl.pallas_call(kernel, out_shape=(pltpu.VMEM((CD, M // PORTS, 2 * M), F32...]
where the time goes in v3:
time: 48.1 us; the launch traced here: 48 us
  Pallas kernels  47.3 us (98%)
  between operations  0.64 us (1%)
    pallas_call x1, Pallas kernels, shards(): pl.pallas_call(kernel, out_shape=(pltpu.VMEM((CD, M // PORTS, 2 * M), F32...  46.4 us

profile of v3, /device:TPU:1, one launch (start us, length us, event | category | flops | bytes accessed | tf_op | source)
XLA Modules:
  0.0 48.0 jit_solution(4084383465113534986)
XLA Ops:
  0.6 46.4 %reduce_components.1 = (f32[16,16,256]{2,1,0:T(8,128)S(1)}, f32[2,256,256]{2,1,0:T(8,128)S(1)}) custom-call(s32[3,8,16]{2,1,0:T(8,128)} %bitcast.8, s32[4,16]{1,0:T(4,128)} %bitcast.9, s32[4,16]{1,0:T(4,128)} %bitcast.11, s32[4,16]{1,0:T(4,128)} %bitcast.10, s32[4,16]{1,0:T(4,128)} %bitcast.12, s32[1,16]{1,0:T(1,128)} %bitcast.13, ...), custom_call_target="tpu_custom_call" | custom-call | tf_op jit(solution)/shard_map/reduce_components/pallas_call | solution.py:464
  47.0 0.9 %finish.1 = (f32[16,16,128]{2,1,0:T(8,128)}, f32[16,16,128]{2,1,0:T(8,128)}, f32[2,256,256]{2,1,0:T(8,128)}) custom-call(f32[16,16,256]{2,1,0:T(8,128)S(1)} %get-tuple-element.5.sums, f32[2,256,256]{2,1,0:T(8,128)S(1)} %get-tuple-element.6.face), custom_call_target="tpu_custom_call" | custom-call | tf_op jit(solution)/shard_map/finish/pallas_call | solution.py:535

commit v4 on v3

--- a/solution.py
+++ b/solution.py
@@ -10,7 +10,7 @@
 CD, NBL, NB, NP = 16, 8, 3, 4
 BS, M, PB = 128, 128, 256
 HOPS = ((0, 1), (0, 3), (1, 0), (3, 0), (1, 1), (3, 3), (1, 3), (3, 1), (2, 0), (0, 2), (2, 3), (2, 1), (3, 2), (1, 2), (2, 2))
-EARLY = 8
+EARLY = 10
 LAST = 3
 AHEAD = 12
 Z_HOPS = (4, 5, 2, 3, 6, 7, 1)

time: 48.1 us -> 48 us (level)
  no operation moved by 1% of the time
where the time goes in v4:
time: 48 us; the launch traced here: 47.8 us
  Pallas kernels  47.2 us (98%)
  between operations  0.64 us (1%)
    pallas_call x1, Pallas kernels, shards(): pl.pallas_call(kernel, out_shape=(pltpu.VMEM((CD, M // PORTS, 2 * M), F32...  46.2 us

profile of v4, /device:TPU:1, one launch (start us, length us, event | category | flops | bytes accessed | tf_op | source)
XLA Modules:
  0.0 47.8 jit_solution(6957782035151175826)
XLA Ops:
  0.6 46.2 %reduce_components.1 = (f32[16,16,256]{2,1,0:T(8,128)S(1)}, f32[2,256,256]{2,1,0:T(8,128)S(1)}) custom-call(s32[3,8,16]{2,1,0:T(8,128)} %bitcast.8, s32[4,16]{1,0:T(4,128)} %bitcast.9, s32[4,16]{1,0:T(4,128)} %bitcast.11, s32[4,16]{1,0:T(4,128)} %bitcast.10, s32[4,16]{1,0:T(4,128)} %bitcast.12, s32[1,16]{1,0:T(1,128)} %bitcast.13, ...), custom_call_target="tpu_custom_call" | custom-call | tf_op jit(solution)/shard_map/reduce_components/pallas_call | solution.py:464
  46.9 0.9 %finish.1 = (f32[16,16,128]{2,1,0:T(8,128)}, f32[16,16,128]{2,1,0:T(8,128)}, f32[2,256,256]{2,1,0:T(8,128)}) custom-call(f32[16,16,256]{2,1,0:T(8,128)S(1)} %get-tuple-element.5.sums, f32[2,256,256]{2,1,0:T(8,128)S(1)} %get-tuple-element.6.face), custom_call_target="tpu_custom_call" | custom-call | tf_op jit(solution)/shard_map/finish/pallas_call | solution.py:535

commit v5 on v4

--- a/solution.py
+++ b/solution.py
@@ -257,11 +257,6 @@
     def send_down(c):
         return remote(shapes.at[pl.ds(c * NBL, 2)], halo_hi.at[c], halo_ss.at[1, c], halo_rs.at[1, c], port=before)
 
-    @pl.loop(0, CD)
-    def _(c):
-        send_up(c).start()
-        send_down(c).start()
-
     def inner(c):
         load_vals(c).wait()
         for r in range(NBL):
@@ -285,7 +280,14 @@
 
     load_cond.wait()
     load_cap.wait()
-    pl.loop(0, AHEAD)(inner)
+    pl.loop(0, 4)(inner)
+
+    @pl.loop(0, CD)
+    def _(c):
+        send_up(c).start()
+        send_down(c).start()
+
+    pl.loop(4, AHEAD)(inner)
 
     @pl.loop(1, PORTS)
     def _(j):

time: 48 us -> 48 us (level)
  no operation moved by 1% of the time
where the time goes in v5:
time: 48 us; the launch traced here: 47.8 us
  Pallas kernels  47.2 us (98%)
  between operations  0.64 us (1%)
    pallas_call x1, Pallas kernels, shards(): pl.pallas_call(kernel, out_shape=(pltpu.VMEM((CD, M // PORTS, 2 * M), F32...  46.2 us

profile of v5, /device:TPU:1, one launch (start us, length us, event | category | flops | bytes accessed | tf_op | source)
XLA Modules:
  0.0 47.8 jit_solution(2120985220061531750)
XLA Ops:
  0.6 46.2 %reduce_components.1 = (f32[16,16,256]{2,1,0:T(8,128)S(1)}, f32[2,256,256]{2,1,0:T(8,128)S(1)}) custom-call(s32[3,8,16]{2,1,0:T(8,128)} %bitcast.8, s32[4,16]{1,0:T(4,128)} %bitcast.9, s32[4,16]{1,0:T(4,128)} %bitcast.11, s32[4,16]{1,0:T(4,128)} %bitcast.10, s32[4,16]{1,0:T(4,128)} %bitcast.12, s32[1,16]{1,0:T(1,128)} %bitcast.13, ...), custom_call_target="tpu_custom_call" | custom-call | tf_op jit(solution)/shard_map/reduce_components/pallas_call | solution.py:466
  46.9 0.9 %finish.1 = (f32[16,16,128]{2,1,0:T(8,128)}, f32[16,16,128]{2,1,0:T(8,128)}, f32[2,256,256]{2,1,0:T(8,128)}) custom-call(f32[16,16,256]{2,1,0:T(8,128)S(1)} %get-tuple-element.5.sums, f32[2,256,256]{2,1,0:T(8,128)S(1)} %get-tuple-element.6.face), custom_call_target="tpu_custom_call" | custom-call | tf_op jit(solution)/shard_map/finish/pallas_call | solution.py:537
